TPU v7x, 32 devices: a whole 2x2x4 slice. The times are simulated.
32 devices in a mesh: dp: 4 (over z), fsdp: 8 (over y, x, core).
Axes of the slice: x: 2, y: 2, z: 4, core: 2. Of those that a mesh axis runs over, the one named last changes fastest.
Arguments:
- dec_in: bfloat16 [64, 176, 768], P(('dp', 'fsdp')), may hold values from -6 to 6
- enc_out: bfloat16 [64, 512, 768], P(('dp', 'fsdp')), may hold values from -6 to 6
- seg_dec: int32 [64, 176], P(('dp', 'fsdp')), may hold values from 0 to 4, as said below
- seg_enc: int32 [64, 512], P(('dp', 'fsdp')), may hold values from 0 to 4, as said below
- out_grad: bfloat16 [64, 176, 768], P(('dp', 'fsdp')), may hold values from -6 to 6
- gain_self: bfloat16 [768], P('fsdp'), may hold values from 0.099609375 to 1.8984375
- wq_self: bfloat16 [768, 768], P('fsdp'), may hold values from -0.21875 to 0.21875
- wk_self: bfloat16 [768, 768], P('fsdp'), may hold values from -0.21875 to 0.21875
- wv_self: bfloat16 [768, 768], P('fsdp'), may hold values from -0.21875 to 0.21875
- wo_self: bfloat16 [768, 768], P('fsdp'), may hold values from -1.5 to 1.5
- gain_cross: bfloat16 [768], P('fsdp'), may hold values from 0.099609375 to 1.8984375
- wq_cross: bfloat16 [768, 768], P('fsdp'), may hold values from -0.21875 to 0.21875
- wk_cross: bfloat16 [768, 768], P('fsdp'), may hold values from -0.21875 to 0.21875
- wv_cross: bfloat16 [768, 768], P('fsdp'), may hold values from -0.21875 to 0.21875
- wo_cross: bfloat16 [768, 768], P('fsdp'), may hold values from -2.5 to 2.5
- gain_ffn: bfloat16 [768], P('fsdp'), may hold values from 0.099609375 to 1.8984375
- w_gate: bfloat16 [768, 2048], P('fsdp'), may hold values from -0.21875 to 0.21875
- w_up: bfloat16 [768, 2048], P('fsdp'), may hold values from -0.21875 to 0.21875
- w_down: bfloat16 [2048, 768], P('fsdp'), may hold values from -0.125 to 0.125
Outputs:
- dec_out: bfloat16 [64, 176, 768], P(('dp', 'fsdp'))
- grad_dec: float32 [64, 176, 768], P(('dp', 'fsdp'))
- grad_enc: float32 [64, 512, 768], P(('dp', 'fsdp'))
- grad_gain_self: float32 [768], P('fsdp')
- grad_wq_self: float32 [768, 768], P('fsdp')
- grad_wk_self: float32 [768, 768], P('fsdp')
- grad_wv_self: float32 [768, 768], P('fsdp')
- grad_wo_self: float32 [768, 768], P('fsdp')
- grad_gain_cross: float32 [768], P('fsdp')
- grad_wq_cross: float32 [768, 768], P('fsdp')
- grad_wk_cross: float32 [768, 768], P('fsdp')
- grad_wv_cross: float32 [768, 768], P('fsdp')
- grad_wo_cross: float32 [768, 768], P('fsdp')
- grad_gain_ffn: float32 [768], P('fsdp')
- grad_w_gate: float32 [768, 2048], P('fsdp')
- grad_w_up: float32 [768, 2048], P('fsdp')
- grad_w_down: float32 [2048, 768], P('fsdp')
Inputs may be any that keep to these rules, and one draw needn't show every extreme that they name: `seg_dec`: each row holds segments 1, 2, 3, 4 in this order, each present in both its decoder and its encoder tokens, then 1 to 176 // 16 (decoder) or 512 // 16 (encoder) padding tokens of segment 0 at its end. `seg_enc`: as for seg_dec, with the same segments present.
All inputs are finite; a program needn't handle non-finite values.
Results may differ from a plain program's by a relative error of at most 0.023.
Values may be sent and summed in bfloat16 or wider, within the bound.
A program may use at most 192 MiB of HBM per device.

v0:
```python
import jax
import jax.numpy as jnp
from jax import lax
from jax.sharding import PartitionSpec as P

HD = 64
EPSILON = 1e-06
MASKED = -1000000000.0


def rms_forward(values_in, gain_vec):
    return (
        values_in
        * lax.rsqrt(jnp.mean(values_in * values_in, axis=-1, keepdims=True) + EPSILON)
        * gain_vec
    )


def rms_backward(values_in, gain_low, grad_out):
    _, pullback = jax.vjp(rms_forward, values_in, gain_low.astype(jnp.float32))
    return pullback(grad_out)


def project(acts, weight):
    return jnp.einsum("rld,dn->rln", acts, weight, preferred_element_type=jnp.float32)


def weight_grad(acts, grad_out):
    return jnp.einsum("rld,rln->dn", acts, grad_out, preferred_element_type=jnp.float32)


def input_grad(grad_out, weight):
    return jnp.einsum("rln,dn->rld", grad_out, weight, preferred_element_type=jnp.float32)


def split_heads(tensor):
    return tensor.reshape(tensor.shape[0], tensor.shape[1], -1, HD)


def merge_heads(tensor):
    return tensor.reshape(tensor.shape[0], tensor.shape[1], -1)


def masked_scores(queries, keys_all, allowed):
    raw_scores = jnp.einsum(
        "rqhd,rkhd->rhqk",
        split_heads(queries),
        split_heads(keys_all),
        preferred_element_type=jnp.float32,
    ) * HD ** (-0.5)
    return jnp.where(allowed[:, None], raw_scores, MASKED)


def attend_forward(queries, keys_all, values, allowed):
    scores = masked_scores(queries, keys_all, allowed)
    maxima = jnp.max(scores, axis=-1, keepdims=True)
    log_total = maxima + jnp.log(jnp.sum(jnp.exp(scores - maxima), axis=-1, keepdims=True))
    weights_low = jnp.exp(scores - log_total).astype(jnp.bfloat16)
    mixture = jnp.einsum(
        "rhqk,rkhd->rqhd", weights_low, split_heads(values), preferred_element_type=jnp.float32
    )
    return (merge_heads(mixture).astype(jnp.bfloat16), log_total)


def attend_backward(queries, keys_all, values, allowed, log_total, grad_mix):
    scores = masked_scores(queries, keys_all, allowed)
    weights_full = jnp.exp(scores - log_total)
    grad_heads = split_heads(grad_mix)
    grad_values = jnp.einsum(
        "rhqk,rqhd->rkhd",
        weights_full.astype(jnp.bfloat16),
        grad_heads,
        preferred_element_type=jnp.float32,
    )
    grad_weights = jnp.einsum(
        "rqhd,rkhd->rhqk", grad_heads, split_heads(values), preferred_element_type=jnp.float32
    )
    grad_scores = (
        weights_full * (grad_weights - jnp.sum(weights_full * grad_weights, axis=-1, keepdims=True))
    ).astype(jnp.bfloat16)
    grad_queries = jnp.einsum(
        "rhqk,rkhd->rqhd", grad_scores, split_heads(keys_all), preferred_element_type=jnp.float32
    ) * HD ** (-0.5)
    grad_keys = jnp.einsum(
        "rhqk,rqhd->rkhd", grad_scores, split_heads(queries), preferred_element_type=jnp.float32
    ) * HD ** (-0.5)
    return (
        merge_heads(grad_queries).astype(jnp.bfloat16),
        merge_heads(grad_keys).astype(jnp.bfloat16),
        merge_heads(grad_values).astype(jnp.bfloat16),
    )


def gather_group(shards):
    joined = jnp.concatenate(shards, axis=0)
    whole = lax.all_gather(joined, "fsdp", axis=0, tiled=False)
    parts = []
    start = 0
    for shard in shards:
        part = whole[:, start : start + shard.shape[0]]
        parts.append(part.reshape((-1,) + shard.shape[1:]))
        start += shard.shape[0]
    return parts


def reduce_group(gradients, shards):
    count = lax.axis_size("fsdp")
    joined = jnp.concatenate(
        [
            gradient.astype(jnp.bfloat16).reshape((count, -1) + gradient.shape[1:])
            for gradient in gradients
        ],
        axis=1,
    )
    owned = lax.psum_scatter(joined, "fsdp", scatter_dimension=0, tiled=False)
    quarter = lax.psum_scatter(owned, "dp", scatter_dimension=0, tiled=True)
    summed = lax.all_gather(quarter, "dp", axis=0, tiled=True)
    parts = []
    start = 0
    for shard in shards:
        part = summed[start : start + shard.shape[0]]
        parts.append(part.astype(jnp.float32))
        start += shard.shape[0]
    return parts


def micro_step(
    dec_rows, enc_rows, seg_rows_dec, seg_rows_enc, grad_rows, get_self, get_cross, get_ffn
):
    position = jnp.arange(seg_rows_dec.shape[1])
    causal = position[:, None] >= position[None, :]
    self_ok = (seg_rows_dec[:, :, None] == seg_rows_dec[:, None, :]) & causal[None]
    cross_ok = seg_rows_dec[:, :, None] == seg_rows_enc[:, None, :]
    gain_a, wq_a, wk_a, wv_a, wo_a = get_self()
    dec_float = dec_rows.astype(jnp.float32)
    normed_a = rms_forward(dec_float, gain_a.astype(jnp.float32)).astype(jnp.bfloat16)
    query_a = project(normed_a, wq_a).astype(jnp.bfloat16)
    keys_a = project(normed_a, wk_a).astype(jnp.bfloat16)
    values_a = project(normed_a, wv_a).astype(jnp.bfloat16)
    mix_a, total_a = attend_forward(query_a, keys_a, values_a, self_ok)
    after_self = dec_float + project(mix_a, wo_a)
    gain_c, wq_c, wk_c, wv_c, wo_c = get_cross()
    normed_c = rms_forward(after_self, gain_c.astype(jnp.float32)).astype(jnp.bfloat16)
    query_c = project(normed_c, wq_c).astype(jnp.bfloat16)
    keys_c = project(enc_rows, wk_c).astype(jnp.bfloat16)
    values_c = project(enc_rows, wv_c).astype(jnp.bfloat16)
    mix_c, total_c = attend_forward(query_c, keys_c, values_c, cross_ok)
    after_cross = after_self + project(mix_c, wo_c)
    gain_f, gate_w, up_w, down_w = get_ffn()
    normed_f = rms_forward(after_cross, gain_f.astype(jnp.float32)).astype(jnp.bfloat16)
    gate_pre = project(normed_f, gate_w)
    up_pre = project(normed_f, up_w)
    hidden_low = (jax.nn.gelu(gate_pre, approximate=True) * up_pre).astype(jnp.bfloat16)
    dec_result = (after_cross + project(hidden_low, down_w)).astype(jnp.bfloat16)
    gain_f, gate_w, up_w, down_w = get_ffn()
    grad_res = grad_rows.astype(jnp.float32)
    grad_branch = grad_res.astype(jnp.bfloat16)
    grad_down = weight_grad(hidden_low, grad_branch)
    grad_hidden = input_grad(grad_branch, down_w)
    _, gelu_pull = jax.vjp(
        lambda gate_in, up_in: jax.nn.gelu(gate_in, approximate=True) * up_in, gate_pre, up_pre
    )
    grad_gate_pre, grad_up_pre = gelu_pull(grad_hidden)
    grad_gate_low = grad_gate_pre.astype(jnp.bfloat16)
    grad_up_low = grad_up_pre.astype(jnp.bfloat16)
    grad_gate = weight_grad(normed_f, grad_gate_low)
    grad_up = weight_grad(normed_f, grad_up_low)
    grad_normed = input_grad(grad_gate_low, gate_w) + input_grad(grad_up_low, up_w)
    grad_input, grad_gain_f = rms_backward(after_cross, gain_f, grad_normed)
    grad_res = grad_res + grad_input
    gain_c, wq_c, wk_c, wv_c, wo_c = get_cross()
    grad_branch = grad_res.astype(jnp.bfloat16)
    grad_wo_c = weight_grad(mix_c, grad_branch)
    grad_mix = input_grad(grad_branch, wo_c).astype(jnp.bfloat16)
    grad_query, grad_keys, grad_values = attend_backward(
        query_c, keys_c, values_c, cross_ok, total_c, grad_mix
    )
    grad_wq_c = weight_grad(normed_c, grad_query)
    grad_wk_c = weight_grad(enc_rows, grad_keys)
    grad_wv_c = weight_grad(enc_rows, grad_values)
    grad_enc_rows = input_grad(grad_keys, wk_c) + input_grad(grad_values, wv_c)
    grad_normed = input_grad(grad_query, wq_c)
    grad_input, grad_gain_c = rms_backward(after_self, gain_c, grad_normed)
    grad_res = grad_res + grad_input
    gain_a, wq_a, wk_a, wv_a, wo_a = get_self()
    grad_branch = grad_res.astype(jnp.bfloat16)
    grad_wo_a = weight_grad(mix_a, grad_branch)
    grad_mix = input_grad(grad_branch, wo_a).astype(jnp.bfloat16)
    grad_query, grad_keys, grad_values = attend_backward(
        query_a, keys_a, values_a, self_ok, total_a, grad_mix
    )
    grad_wq_a = weight_grad(normed_a, grad_query)
    grad_wk_a = weight_grad(normed_a, grad_keys)
    grad_wv_a = weight_grad(normed_a, grad_values)
    grad_normed = (
        input_grad(grad_query, wq_a) + input_grad(grad_keys, wk_a) + input_grad(grad_values, wv_a)
    )
    grad_input, grad_gain_a = rms_backward(dec_float, gain_a, grad_normed)
    grad_dec_rows = grad_res + grad_input
    full_grads = (
        grad_gain_a,
        grad_wq_a,
        grad_wk_a,
        grad_wv_a,
        grad_wo_a,
        grad_gain_c,
        grad_wq_c,
        grad_wk_c,
        grad_wv_c,
        grad_wo_c,
        grad_gain_f,
        grad_gate,
        grad_up,
        grad_down,
    )
    return (dec_result, grad_dec_rows, grad_enc_rows, full_grads)


def body(
    dec_in,
    enc_out,
    seg_dec,
    seg_enc,
    out_grad,
    gain_self,
    wq_self,
    wk_self,
    wv_self,
    wo_self,
    gain_cross,
    wq_cross,
    wk_cross,
    wv_cross,
    wo_cross,
    gain_ffn,
    w_gate,
    w_up,
    w_down,
):
    narrow = (wq_self, wk_self, wv_self, wo_self, wq_cross, wk_cross, wv_cross, wo_cross, w_down)
    gain_a, gain_c, gain_f = gather_group((gain_self, gain_cross, gain_ffn))
    full = gather_group(narrow)
    gate_full, up_full = gather_group((w_gate, w_up))
    get_self = lambda: (gain_a, *full[0:4])
    get_cross = lambda: (gain_c, *full[4:8])
    get_ffn = lambda: (gain_f, gate_full, up_full, full[8])
    result_rows, grad_rows_dec, grad_rows_enc, grads = micro_step(
        dec_in, enc_out, seg_dec, seg_enc, out_grad, get_self, get_cross, get_ffn
    )
    gains = reduce_group((grads[0], grads[5], grads[10]), (gain_self, gain_cross, gain_ffn))
    wide = reduce_group(grads[11:13], (w_gate, w_up))
    thin = reduce_group(grads[1:5] + grads[6:10] + grads[13:14], narrow)
    return (
        (result_rows, grad_rows_dec, grad_rows_enc, gains[0])
        + tuple(thin[0:4])
        + (gains[1],)
        + tuple(thin[4:8])
        + (gains[2], *wide, thin[8])
    )


def solution(mesh):
    placed = (
        P(("dp", "fsdp"), None, None),
        P(("dp", "fsdp"), None, None),
        P(("dp", "fsdp"), None),
        P(("dp", "fsdp"), None),
        P(("dp", "fsdp"), None, None),
        P("fsdp"),
        P("fsdp", None),
        P("fsdp", None),
        P("fsdp", None),
        P("fsdp", None),
        P("fsdp"),
        P("fsdp", None),
        P("fsdp", None),
        P("fsdp", None),
        P("fsdp", None),
        P("fsdp"),
        P("fsdp", None),
        P("fsdp", None),
        P("fsdp", None),
    )
    return jax.shard_map(
        body,
        mesh=mesh,
        in_specs=placed,
        out_specs=(
            P(("dp", "fsdp"), None, None),
            P(("dp", "fsdp"), None, None),
            P(("dp", "fsdp"), None, None),
            P("fsdp"),
            P("fsdp", None),
            P("fsdp", None),
            P("fsdp", None),
            P("fsdp", None),
            P("fsdp"),
            P("fsdp", None),
            P("fsdp", None),
            P("fsdp", None),
            P("fsdp", None),
            P("fsdp"),
            P("fsdp", None),
            P("fsdp", None),
            P("fsdp", None),
        ),
        check_vma=False,
    )
```

profile of v0, /device:TPU:0, one launch (start us, length us, event | category | flops | bytes accessed | tf_op | source)
XLA Modules:
  0.0 545.3 jit_solution(10635128616492890739)
XLA Ops:
  7.3 2.2 pad_maximum_fusion.1
  17.5 16.0 %all-reduce = bf16[2304]{0:T(1024)(128)(2,1)S(1)} all-reduce(bf16[2304]{0:T(1024)(128)(2,1)S(1)} %dynamic-update-slice), channel_id=2, replica_groups=mesh['dp'=4,'fsdp'=8] {'fsdp'}, use_global_device_ids=true, to_apply=%add | all-reduce | flops 2304 | bytes 9216
  35.1 24.0 %all-gather.11.cloned.1.call-done = bf16[1536,2048]{1,0:T(8,128)(2,1)} async-done(((bf16[192,2048]{1,0:T(8,128)(2,1)}), bf16[1536,2048]{1,0:T(8,128)(2,1)}) %all-gather.11.cloned.1.call-update) | async-done | bytes 6291472 | tf_op jit(solution)/shard_map/all_gather | solution.py:96
  59.1 6.7 %fusion.43 = (bf16[8,96,2048]{2,1,0:T(8,128)(2,1)}, bf16[8,96,2048]{2,1,0:T(8,128)(2,1)}) fusion(bf16[8,192,2048]{2,1,0:T(8,128)(2,1)} %bitcast.212), kind=kLoop, calls=%fused_computation.149 | loop fusion | bytes 12582912 | tf_op jit(solution)/shard_map/slice | solution.py:100
  65.8 67.4 %all-gather.9.cloned.1.call-done = bf16[8192,768]{1,0:T(8,128)(2,1)} async-done(((bf16[1024,768]{1,0:T(8,128)(2,1)}), bf16[8192,768]{1,0:T(8,128)(2,1)}) %all-gather.9.cloned.1.call-update) | async-done | bytes 12582928 | tf_op jit(solution)/shard_map/all_gather | solution.py:96
  133.1 3.8 slice.125
  136.9 6.9 %fusion.42 = (bf16[8,96,768]{2,1,0:T(8,128)(2,1)}, bf16[8,96,768]{2,1,0:T(8,128)(2,1)}, bf16[8,96,768]{2,1,0:T(8,128)(2,1)}, bf16[8,96,768]{2,1,0:T(8,128)(2,1)}...) fusion(bf16[8,1024,768]{2,1,0:T(8,128)(2,1)} %bitcast.197), kind=kLoop, calls=%fused_computation.148 | loop fusion | bytes 18874368 | tf_op jit(solution)/shard_map/slice | solution.py:100
  145.8 2.7 convolution_convert_fusion.10
  148.5 1.3 copy.105
  149.8 3.2 convolution_convert_fusion.11
  153.0 2.2 copy.104
  155.2 3.9 convolution_convert_fusion.1
  159.2 2.6 convolution_convert_fusion.2
  167.7 1.5 convolution_convert_fusion.8
  169.1 2.2 copy.110
  171.3 3.5 fusion
  174.9 3.2 exponential_reduce_fusion
  178.3 2.6 convolution_convert_fusion.3
  181.8 1.3 copy-done.3
  187.1 4.7 multiply_convert_fusion.3
  191.7 1.4 fusion.48
  193.4 2.1 multiply_reduce_fusion.2
  195.9 1.4 convolution_convert_fusion.7
  197.3 1.9 bitcast_convert_fusion.3
  199.2 2.2 copy.113
  201.5 7.2 %convolution_convert_fusion = bf16[2,12,64,512]{3,2,1,0:T(8,128)(2,1)} fusion(bf16[2,176,12,64]{1,3,2,0:T(8,128)(2,1)} %bitcast.225, f32[2,12,176,512]{3,2,1,0:T(8,128)} %copy-done.1, f32[2,12,176]{2,1,0:T(8,128)} %copy-done.55, pred[2,176,512]{2,1,0:T(8,128)(4,1)} %broadcast_compare_fusion), kind=kOutput, calls=%fused_computation.46 | convolution fusion | flops 286261248 | bytes 10961408 | tf_op jit(solution)/shard_map/rhqk,rqhd->rkhd/dot_general | solution.py:69
  208.7 5.9 %multiply_reduce_fusion = (f32[2,12,176]{2,1,0:T(8,128)S(1)}, f32[2,12,176,512]{3,2,1,0:T(8,128)S(1)}) fusion(f32[2,12,176,512]{3,2,1,0:T(8,128)} %copy-done.1, f32[2,12,176]{2,1,0:T(8,128)S(1)} %copy-done.56, pred[2,176,512]{2,1,0:T(8,128)(4,1)S(1)} %copy-done.30, bf16[2,176,12,64]{1,3,2,0:T(8,128)(2,1)S(1)} %bitcast.226, ...), kind=kOutput, calls=%fused_computation.1 | convolution fusion | flops 287633280 | bytes 19629056 | tf_op jit(solution)/shard_map/rqhd,rkhd->rhqk/dot_general | solution.py:75
  214.7 2.7 multiply_convert_fusion
  217.5 1.5 multiply_convert_fusion.7
  219.0 2.1 multiply_convert_fusion.2
  221.1 1.5 multiply_reduce_fusion.3
  222.6 2.0 bitcast_convert_fusion.6
  225.9 1.4 convolution_convert_fusion.6
  227.4 1.9 bitcast_convert_fusion.7
  229.2 1.3 copy.115
  230.6 3.5 convolution_convert_fusion.4
  234.1 4.1 multiply_reduce_fusion.1
  238.3 1.3 multiply_convert_fusion.1
  241.0 1.4 copy-done.43
  242.4 1.5 bitcast_convert_fusion.4
  244.0 2.1 bitcast_convert_fusion.2
  247.5 1.5 bitcast_convert_fusion.5
  261.0 1.9 constant_dynamic-update-slice_fusion.9
  263.9 3.3 bitcast_convert_fusion
  267.2 1.8 bitcast_convert_fusion.1
  269.1 4.9 pad_maximum_fusion
  274.1 81.4 %reduce-scatter.5.cloned.1.call-done = bf16[1,1024,768]{2,1,0:T(8,128)(2,1)} async-done(((bf16[8,1024,768]{2,1,0:T(8,128)(2,1)}), bf16[1,1024,768]{2,1,0:T(8,128)(2,1)}) %reduce-scatter.5.cloned.1.call-update) | async-done | bytes 1572880 | tf_op jit(solution)/shard_map/reduce_scatter | solution.py:115
  355.5 64.9 %reduce-scatter.9.cloned.1.call-done = bf16[1,192,2048]{2,1,0:T(8,128)(2,1)} async-done(((bf16[8,192,2048]{2,1,0:T(8,128)(2,1)}), bf16[1,192,2048]{2,1,0:T(8,128)(2,1)}) %reduce-scatter.9.cloned.1.call-update) | async-done | bytes 786448 | tf_op jit(solution)/shard_map/reduce_scatter | solution.py:115
  422.2 2.2 fusion.49
  424.5 2.2 convolution_add_fusion.2
  426.7 1.9 fusion.15
  428.8 2.5 fusion.18
  431.3 26.7 %reduce-scatter.7.cloned.1.call-done = bf16[256,768]{1,0:T(8,128)(2,1)} async-done(((bf16[1024,768]{1,0:T(8,128)(2,1)}), bf16[256,768]{1,0:T(8,128)(2,1)}) %reduce-scatter.7.cloned.1.call-update) | async-done | bytes 393232 | tf_op jit(solution)/shard_map/reduce_scatter | solution.py:116
  458.1 13.7 %all-reduce.2 = bf16[8,288]{1,0:T(8,128)(2,1)S(1)} all-reduce(bf16[8,288]{1,0:T(8,128)(2,1)S(1)} %pad_maximum_fusion.2), channel_id=5, replica_groups=mesh['dp'=4,'fsdp'=8] {'fsdp'}, use_global_device_ids=true, to_apply=%region_15.16.clone | all-reduce | flops 2304 | bytes 9216
  472.5 10.3 %all-reduce.3 = bf16[288]{0:T(512)(128)(2,1)S(1)} all-reduce(bf16[288]{0:T(512)(128)(2,1)S(1)} %dynamic-slice_reduce_fusion), channel_id=6, replica_groups=mesh['dp'=4,'fsdp'=8] {'dp'}, use_global_device_ids=true, to_apply=%region_16.17.clone | all-reduce | flops 288 | bytes 1152
  483.1 8.6 %all-reduce.1 = bf16[288]{0:T(512)(128)(2,1)S(1)} all-reduce(bf16[288]{0:T(512)(128)(2,1)S(1)} %dynamic-update-slice.1), channel_id=1, replica_groups=mesh['dp'=4,'fsdp'=8] {'dp'}, use_global_device_ids=true, to_apply=%add.1 | all-reduce | flops 288 | bytes 1152
  492.3 3.3 fusion.50
  495.8 2.1 fusion.11
  497.9 3.1 convolution_add_fusion
  501.0 28.7 %all_gather.35 = bf16[192,2048]{1,0:T(8,128)(2,1)S(1)} all-gather(bf16[48,2048]{1,0:T(8,128)(2,1)} %reduce-scatter.11.cloned.1.call-done), channel_id=1, replica_groups=mesh['dp'=4,'fsdp'=8] {'dp'}, dimensions={0}, use_global_device_ids=true | all-gather | bytes 983040 | tf_op jit(solution)/shard_map/all_gather | solution.py:117
  529.7 1.3 slice_convert_fusion.1
  531.1 2.4 all-gather.7.cloned.1.call-done
  533.5 1.9 slice_convert_fusion
  535.4 2.8 slice_convert_fusion.3
  (255 shorter events, 41.9 us)
Async XLA Ops:
  7.2 148.0 %copy-start = (bf16[2,512,768]{2,1,0:T(8,128)(2,1)S(1)}, bf16[2,512,768]{2,1,0:T(8,128)(2,1)}, u32[]{:S(2)}) copy-start(bf16[2,512,768]{2,1,0:T(8,128)(2,1)} %param.20) | copy-start | bytes 4718596
  7.2 2.4 copy-start.57
  7.2 3.1 copy-start.58
  7.2 3.7 copy-start.59
  7.2 4.4 copy-start.60
  7.2 5.1 copy-start.61
  7.3 5.7 %copy-start.62 = (bf16[96,768]{1,0:T(8,128)(2,1)S(1)}, bf16[96,768]{1,0:T(8,128)(2,1)}, u32[]{:S(2)}) copy-start(bf16[96,768]{1,0:T(8,128)(2,1)} %param.31) | copy-start | bytes 442372
  7.3 51.8 %all-gather.11.cloned.1.call-start = ((), (), s32[]{:S(2)}) async-start(), calls=%async_computation.10 | async-start | bytes 7077888 | tf_op jit(solution)/shard_map/all_gather | solution.py:96
  9.5 4.1 copy-start.63
  9.5 4.8 copy-start.64
  9.5 5.5 %copy-start.52 = (bf16[256,768]{1,0:T(8,128)(2,1)S(1)}, bf16[256,768]{1,0:T(8,128)(2,1)}, u32[]{:S(2)}) copy-start(bf16[256,768]{1,0:T(8,128)(2,1)} %param.37) | copy-start | bytes 1179652
  9.6 123.6 %all-gather.9.cloned.1.call-start = ((), (), s32[]{:S(2)}) async-start(), calls=%async_computation.9 | async-start | bytes 14155776 | tf_op jit(solution)/shard_map/all_gather | solution.py:96
  13.0 2.9 copy-start.70
  13.0 2.9 copy-start.71
  13.0 4.2 copy-start.73
  13.0 4.2 copy-start.74
  13.0 4.2 copy-start.75
  13.7 20.2 %copy-start.20 = (bf16[2,176,768]{2,1,0:T(8,128)(2,1)S(1)}, bf16[2,176,768]{2,1,0:T(8,128)(2,1)}, u32[]{:S(2)}) copy-start(bf16[2,176,768]{2,1,0:T(8,128)(2,1)} %param.19) | copy-start | bytes 1622020
  15.0 19.0 %copy-start.65 = (s32[2,176]{1,0:T(2,128)S(1)}, s32[2,176]{1,0:T(2,128)}, u32[]{:S(2)}) copy-start(s32[2,176]{1,0:T(2,128)} %param.21) | copy-start | bytes 4228
  15.0 19.2 %copy-start.69 = (s32[2,512]{1,0:T(2,128)S(1)}, s32[2,512]{1,0:T(2,128)}, u32[]{:S(2)}) copy-start(s32[2,512]{1,0:T(2,128)} %param.22) | copy-start | bytes 12292
  15.8 339.6 %reduce-scatter.5.cloned.1.call-start = ((), (), s32[]{:S(2)}) async-start(), calls=%async_computation.4 | async-start | bytes 14155776 | tf_op jit(solution)/shard_map/reduce_scatter | solution.py:115
  149.8 11.9 %copy-start.14 = (bf16[2,176,768]{1,2,0:T(8,128)(2,1)}, bf16[2,176,768]{1,2,0:T(8,128)(2,1)S(1)}, u32[]{:S(2)}) copy-start(bf16[2,176,768]{1,2,0:T(8,128)(2,1)S(1)} %copy.105) | copy-start | bytes 1622020
  155.2 3.9 copy-start.23
  162.7 2.1 copy-start.2
  162.7 2.1 copy-start.34
  163.8 2.3 copy-start.53
  171.3 3.5 copy-start.29
  174.8 3.4 copy-start.1
  174.8 3.4 copy-start.40
  178.1 2.8 copy-start.55
  178.3 2.6 copy-start.7
  180.9 2.3 copy-start.3
  181.6 13.9 %copy-start.8 = (f32[2,176,768]{2,1,0:T(8,128)}, f32[2,176,768]{2,1,0:T(8,128)S(1)}, u32[]{:S(2)}) copy-start(f32[2,176,768]{2,1,0:T(8,128)S(1)} %get-tuple-element.63) | copy-start | bytes 3244036
  181.8 2.6 copy-start.18
  201.4 7.3 %copy-start.30 = (pred[2,176,512]{2,1,0:T(8,128)(4,1)S(1)}, pred[2,176,512]{2,1,0:T(8,128)(4,1)}, u32[]{:S(2)}) copy-start(pred[2,176,512]{2,1,0:T(8,128)(4,1)} %broadcast_compare_fusion) | copy-start | bytes 540676
  201.4 7.3 %copy-start.31 = (bf16[2,176,768]{1,2,0:T(8,128)(2,1)S(1)}, bf16[2,176,768]{1,2,0:T(8,128)(2,1)}, u32[]{:S(2)}) copy-start(bf16[2,176,768]{1,2,0:T(8,128)(2,1)} %copy.113) | copy-start | bytes 1622020
  201.4 7.3 %copy-start.41 = (bf16[768,2,512]{2,0,1:T(8,128)(2,1)S(1)}, bf16[768,2,512]{2,0,1:T(8,128)(2,1)}, u32[]{:S(2)}) copy-start(bf16[768,2,512]{2,0,1:T(8,128)(2,1)} %convolution_convert_fusion.2) | copy-start | bytes 4718596
  201.4 7.3 %copy-start.56 = (f32[2,12,176]{2,1,0:T(8,128)S(1)}, f32[2,12,176]{2,1,0:T(8,128)}, u32[]{:S(2)}) copy-start(f32[2,12,176]{2,1,0:T(8,128)} %copy-done.55) | copy-start | bytes 50692
  201.4 13.2 %slice-start = ((s8[8650752]{0:T(1024)(128)(4,1)}), s8[4194304]{0:T(1024)(128)(4,1)S(1)}, s32[]{:S(2)}) async-start(s8[8650752]{0:T(1024)(128)(4,1)} %bitcast.192), calls=%async_computation.11 | async-start | bytes 8388608
  201.5 13.2 %slice-start.1 = ((s8[8650752]{0:T(1024)(128)(4,1)}), s8[4194304]{0:T(1024)(128)(4,1)S(1)}, s32[]{:S(2)}) async-start(s8[8650752]{0:T(1024)(128)(4,1)} %bitcast.192), calls=%async_computation.12 | async-start | bytes 8388608
  208.7 6.0 %slice-start.2 = ((s8[8650752]{0:T(1024)(128)(4,1)}), s8[262144]{0:T(1024)(128)(4,1)S(1)}, s32[]{:S(2)}) async-start(s8[8650752]{0:T(1024)(128)(4,1)} %bitcast.192), calls=%async_computation.13 | async-start | bytes 524288
  214.7 2.7 copy-start.17
  227.4 3.2 copy-start.54
  230.6 3.5 copy-start.35
  230.6 7.7 %slice-start.3 = ((s8[4325376]{0:T(1024)(128)(4,1)}), s8[4194304]{0:T(1024)(128)(4,1)S(1)}, s32[]{:S(2)}) async-start(s8[4325376]{0:T(1024)(128)(4,1)} %bitcast.194), calls=%async_computation.14 | async-start | bytes 8388608
  234.1 11.9 %copy-start.48 = (bf16[2,12,64,176]{3,2,1,0:T(8,128)(2,1)}, bf16[2,12,64,176]{3,2,1,0:T(8,128)(2,1)S(1)}, u32[]{:S(2)}) copy-start(bf16[2,12,64,176]{3,2,1,0:T(8,128)(2,1)S(1)} %convolution_convert_fusion.4) | copy-start | bytes 1622020
  234.1 4.1 slice-start.4
  240.5 8.5 %copy-start.38 = (bf16[2,12,64,176]{3,2,1,0:T(8,128)(2,1)}, bf16[2,12,64,176]{3,2,1,0:T(8,128)(2,1)S(1)}, u32[]{:S(2)}) copy-start(bf16[2,12,64,176]{3,2,1,0:T(8,128)(2,1)S(1)} %multiply_convert_fusion.5) | copy-start | bytes 1622020
  241.0 8.9 %copy-start.36 = (bf16[2,12,64,176]{3,2,1,0:T(8,128)(2,1)}, bf16[2,12,64,176]{3,2,1,0:T(8,128)(2,1)S(1)}, u32[]{:S(2)}) copy-start(bf16[2,12,64,176]{3,2,1,0:T(8,128)(2,1)S(1)} %multiply_convert_fusion.6) | copy-start | bytes 1622020
  262.9 157.5 %reduce-scatter.9.cloned.1.call-start = ((), (), s32[]{:S(2)}) async-start(), calls=%async_computation.7 | async-start | bytes 7077888 | tf_op jit(solution)/shard_map/reduce_scatter | solution.py:115
  263.9 3.3 copy-start.82
  274.0 148.0 %copy-start.72 = (bf16[768]{0:T(1024)(128)(2,1)S(1)}, bf16[768]{0:T(1024)(128)(2,1)}, u32[]{:S(2)}) copy-start(bf16[768]{0:T(1024)(128)(2,1)} %get-tuple-element.19) | copy-start | bytes 4612
  274.0 148.1 %copy-start.66 = (bf16[768]{0:T(1024)(128)(2,1)S(1)}, bf16[768]{0:T(1024)(128)(2,1)}, u32[]{:S(2)}) copy-start(bf16[768]{0:T(1024)(128)(2,1)} %get-tuple-element.17) | copy-start | bytes 4612
  274.0 148.2 %copy-start.37 = (bf16[2,12,64,176]{3,2,1,0:T(8,128)(2,1)S(1)}, bf16[2,12,64,176]{3,2,1,0:T(8,128)(2,1)}, u32[]{:S(2)}) copy-start(bf16[2,12,64,176]{3,2,1,0:T(8,128)(2,1)} %copy-done.36) | copy-start | bytes 1622020
  274.0 184.0 %reduce-scatter.7.cloned.1.call-start = ((), (), s32[]{:S(2)}) async-start(), calls=%async_computation.5 | async-start | bytes 1966080 | tf_op jit(solution)/shard_map/reduce_scatter | solution.py:116
  355.5 145.5 %reduce-scatter.11.cloned.1.call-start = ((), (), s32[]{:S(2)}) async-start(), calls=%async_computation.8 | async-start | bytes 983040 | tf_op jit(solution)/shard_map/reduce_scatter | solution.py:116
  420.5 113.0 %all-gather.7.cloned.1.call-start = ((), (), s32[]{:S(2)}) async-start(), calls=%async_computation.6 | async-start | bytes 1966080 | tf_op jit(solution)/shard_map/all_gather | solution.py:117
  422.2 2.2 copy-start.39
  424.4 2.3 copy-start.25
  424.4 2.3 copy-start.49
  492.3 3.3 copy-start.9
  492.3 3.3 copy-start.33
  492.3 3.5 copy-start.80
  495.8 2.1 copy-start.44
  (31 other events, 48.9 us)
Sparse Core Ops, SparseCore 0:
  10.6 48.4 all-gather.10
  61.0 72.1 all-gather.8
  263.0 92.3 reduce-scatter.4
  358.7 61.7 reduce-scatter.8
  422.7 35.2 reduce-scatter.6
  460.3 22.3 reduce-scatter.10
  484.3 49.0 all-gather.6
where the time goes:
time: 549 us; the launch traced here: 545 us
  waiting for transfers between devices  267 us (49%)
  matrix products  98.7 us (18%)
  blocking collectives  77.3 us (14%)
  local copies, waits for them, and re-layouts  57.7 us (11%)
  other arithmetic  26.8 us (5%)
  between operations  17.4 us (3%)
    reduce_scatter x2, waiting for transfers between devices, reduce_group(): owned = lax.psum_scatter(joined, 'fsdp', scatter_dimension=0, tiled=False)  146 us
    all_gather x2, waiting for transfers between devices, gather_group(): whole = lax.all_gather(joined, 'fsdp', axis=0, tiled=False)  91.4 us
    unnamed x4, blocking collectives  48.6 us
    all_gather x1, blocking collectives, reduce_group(): summed = lax.all_gather(quarter, 'dp', axis=0, tiled=True)  28.7 us
    unnamed x198, local copies, waits for them, and re-layouts  26.9 us
    reduce_scatter x2, waiting for transfers between devices, reduce_group(): quarter = lax.psum_scatter(owned, 'dp', scatter_dimension=0, tiled=True)  26.7 us
    dot_general x11, matrix products, input_grad(): jnp.einsum('rln,dn->rld', grad_out, weight, preferred_element_type=jnp.fl...  25.4 us
    dot_general x11, matrix products, project(): jnp.einsum('rld,dn->rln', acts, weight, preferred_element_type=jnp.float32)  20.7 us
  transfers between devices with their start and end apart: 7, of which 6 were waited for; matrix products, arithmetic and copies ran while one was open for 8% of the time, Pallas kernels for 0%

commit v1 on v0

--- a/solution.py
+++ b/solution.py
@@ -6,6 +6,19 @@
 HD = 64
 EPSILON = 1e-06
 MASKED = -1000000000.0
+
+
+def columns_push(matrix):
+    local_now = lax.axis_size("dp")
+    latest, side_arr, z_new = (local_now, lax.axis_index("dp"), matrix.shape[0])
+    outer, state_now = (matrix, 1)
+    while state_now < latest:
+        y = map(lambda i: (i, (i - state_now) % latest), range(latest))
+        block_next = list(y)
+        outer = jnp.concatenate([outer, lax.ppermute(outer, "dp", block_next)], 0)
+        state_now = 2 * state_now
+    w2 = jnp.roll(outer, side_arr * z_new, 0)
+    return w2
 
 
 def rms_forward(values_in, gain_vec):
@@ -114,7 +127,7 @@
     )
     owned = lax.psum_scatter(joined, "fsdp", scatter_dimension=0, tiled=False)
     quarter = lax.psum_scatter(owned, "dp", scatter_dimension=0, tiled=True)
-    summed = lax.all_gather(quarter, "dp", axis=0, tiled=True)
+    summed = columns_push(quarter)
     parts = []
     start = 0
     for shard in shards:

time: 549 us -> 520 us (0.947)
  blocking collectives: 77.3 us -> 41 us
  waiting for transfers between devices: 267 us -> 254 us
  starting transfers between devices: 0.53 us -> 13.1 us
  local copies, waits for them, and re-layouts: 57.7 us -> 69 us
  matrix products: 98.7 us -> 93.2 us
    ppermute x0 -> x6, waiting for transfers between devices: none -> 63.2 us  [columns_push(): outer = jnp.concatenate([outer, lax.ppermute(outer, 'dp', block_next)], 0)]
    reduce_scatter x2, waiting for transfers between devices: 146 us -> 93.9 us  [reduce_group(): owned = lax.psum_scatter(joined, 'fsdp', scatter_dimension=0, tiled=False)]
    all_gather x1 -> x0, blocking collectives: 28.7 us -> none  [reduce_group(): summed = lax.all_gather(quarter, 'dp', axis=0, tiled=True)]
    reduce_scatter x2, waiting for transfers between devices: 26.7 us -> 5.89 us  [reduce_group(): quarter = lax.psum_scatter(owned, 'dp', scatter_dimension=0, tiled=True)]
    ppermute x0 -> x6, starting transfers between devices: none -> 12.9 us  [columns_push(): outer = jnp.concatenate([outer, lax.ppermute(outer, 'dp', block_next)], 0)]
    unnamed x198 -> x225, local copies, waits for them, and re-layouts: 26.9 us -> 35.2 us
    unnamed x4 -> x3, blocking collectives: 48.6 us -> 41 us
    dot_general x2, matrix products: 10.7 us -> 3.76 us  [attend_backward(): jnp.einsum('rhqk,rqhd->rkhd', weights_full.astype(jnp.bfloat16), grad_hea...]
  transfers between devices with their start and end apart: 7 -> 12, of which waited for: 6 -> 10; matrix products, arithmetic and copies ran while one was open for 8% -> 18% of each run, Pallas kernels for 0% -> 0%
where the time goes in v1:
time: 520 us; the launch traced here: 516 us
  waiting for transfers between devices  254 us (49%)
  matrix products  93.2 us (18%)
  local copies, waits for them, and re-layouts  69 us (13%)
  blocking collectives  41 us (8%)
  other arithmetic  28.1 us (5%)
  between operations  17 us (3%)
  starting transfers between devices  13.1 us (3%)
    reduce_scatter x2, waiting for transfers between devices, reduce_group(): owned = lax.psum_scatter(joined, 'fsdp', scatter_dimension=0, tiled=False)  93.9 us
    all_gather x2, waiting for transfers between devices, gather_group(): whole = lax.all_gather(joined, 'fsdp', axis=0, tiled=False)  91.3 us
    ppermute x6, waiting for transfers between devices, columns_push(): outer = jnp.concatenate([outer, lax.ppermute(outer, 'dp', block_next)], 0)  63.2 us
    unnamed x3, blocking collectives  41 us
    unnamed x225, local copies, waits for them, and re-layouts  35.2 us
    dot_general x11, matrix products, input_grad(): jnp.einsum('rln,dn->rld', grad_out, weight, preferred_element_type=jnp.fl...  26.5 us
    dot_general x11, matrix products, project(): jnp.einsum('rld,dn->rln', acts, weight, preferred_element_type=jnp.float32)  21.6 us
    slice x3, local copies, waits for them, and re-layouts, gather_group(): part = whole[:, start:start + shard.shape[0]]  17.4 us
  transfers between devices with their start and end apart: 12, of which 10 were waited for; matrix products, arithmetic and copies ran while one was open for 18% of the time, Pallas kernels for 0%

profile of v1, /device:TPU:0, one launch (start us, length us, event | category | flops | bytes accessed | tf_op | source)
XLA Modules:
  0.0 515.8 jit_solution(14804895855744150378)
XLA Ops:
  7.3 2.2 pad_maximum_fusion.1
  17.5 15.9 %all-reduce = bf16[2304]{0:T(1024)(128)(2,1)S(1)} all-reduce(bf16[2304]{0:T(1024)(128)(2,1)S(1)} %dynamic-update-slice), channel_id=2, replica_groups=mesh['dp'=4,'fsdp'=8] {'fsdp'}, use_global_device_ids=true, to_apply=%add | all-reduce | flops 2304 | bytes 9216
  35.1 24.0 %all-gather.8.cloned.1.call-done = bf16[1536,2048]{1,0:T(8,128)(2,1)} async-done(((bf16[192,2048]{1,0:T(8,128)(2,1)}), bf16[1536,2048]{1,0:T(8,128)(2,1)}) %all-gather.8.cloned.1.call-update) | async-done | bytes 6291472 | tf_op jit(solution)/shard_map/all_gather | solution.py:109
  59.1 6.8 %fusion.43 = (bf16[8,96,2048]{2,1,0:T(8,128)(2,1)}, bf16[8,96,2048]{2,1,0:T(8,128)(2,1)}) fusion(bf16[8,192,2048]{2,1,0:T(8,128)(2,1)} %bitcast.215), kind=kLoop, calls=%fused_computation.164 | loop fusion | bytes 12582912 | tf_op jit(solution)/shard_map/slice | solution.py:113
  65.8 67.3 %all-gather.6.cloned.1.call-done = bf16[8192,768]{1,0:T(8,128)(2,1)} async-done(((bf16[1024,768]{1,0:T(8,128)(2,1)}), bf16[8192,768]{1,0:T(8,128)(2,1)}) %all-gather.6.cloned.1.call-update) | async-done | bytes 12582928 | tf_op jit(solution)/shard_map/all_gather | solution.py:109
  133.1 3.7 slice.125
  136.9 7.0 %fusion.42 = (bf16[8,96,768]{2,1,0:T(8,128)(2,1)}, bf16[8,96,768]{2,1,0:T(8,128)(2,1)}, bf16[8,96,768]{2,1,0:T(8,128)(2,1)}, bf16[8,96,768]{2,1,0:T(8,128)(2,1)}...) fusion(bf16[8,1024,768]{2,1,0:T(8,128)(2,1)} %bitcast.200), kind=kLoop, calls=%fused_computation.163 | loop fusion | bytes 18874368 | tf_op jit(solution)/shard_map/slice | solution.py:113
  144.8 1.4 convolution_convert_fusion.9
  146.3 1.3 copy.106
  147.6 3.0 convolution_convert_fusion.10
  150.6 1.3 copy.105
  151.9 2.9 convolution_convert_fusion.11
  154.8 2.2 copy.104
  157.0 4.0 convolution_convert_fusion.1
  161.0 2.6 convolution_convert_fusion.2
  169.4 1.5 convolution_convert_fusion.8
  170.8 2.2 copy.110
  173.0 3.5 fusion
  176.6 3.2 exponential_reduce_fusion
  180.0 2.6 convolution_convert_fusion.3
  183.6 1.5 copy-done.4
  189.0 4.7 multiply_convert_fusion.3
  193.7 1.4 fusion.47
  195.1 3.5 bitcast_convert_fusion.1
  198.6 3.5 bitcast_convert_fusion
  202.1 2.1 multiply_reduce_fusion.2
  205.6 1.4 convolution_convert_fusion.7
  207.1 2.2 copy.113
  209.3 6.6 %pad_maximum_fusion = bf16[8,192,2048]{2,1,0:T(8,128)(2,1)} fusion(bf16[8,96,2048]{2,1,0:T(8,128)(2,1)} %bitcast.242, bf16[8,96,2048]{2,1,0:T(8,128)(2,1)} %bitcast.241), kind=kLoop, calls=%fused_computation.6 | loop fusion | flops 12582912 | bytes 12582912 | tf_op jit(solution)/shard_map/concatenate | solution.py:121
  215.9 7.7 %multiply_reduce_fusion = (f32[2,12,176]{2,1,0:T(8,128)S(1)}, f32[2,12,176,512]{3,2,1,0:T(8,128)S(1)}) fusion(f32[2,12,176,512]{3,2,1,0:T(8,128)} %copy-done.1, f32[2,12,176]{2,1,0:T(8,128)} %copy-done.59, pred[2,176,512]{2,1,0:T(8,128)(4,1)} %broadcast_compare_fusion, bf16[2,176,12,64]{1,3,2,0:T(8,128)(2,1)} %bitcast.228, bf16[2,512,12,64]{1,3,2,0:T(8,128)(2,1)} %bitcast.245), kind=kOutput, calls=%fused_computation.1 | convolution fusion | flops 287633280 | bytes 19629056 | tf_op jit(solution)/shard_map/rqhd,rkhd->rhqk/dot_general | solution.py:88
  223.7 2.7 multiply_convert_fusion
  226.5 1.5 multiply_convert_fusion.7
  228.8 1.5 multiply_reduce_fusion.3
  231.9 1.4 convolution_convert_fusion.6
  233.3 2.2 copy.115
  235.5 4.4 multiply_reduce_fusion.1
  240.0 1.4 multiply_convert_fusion.1
  257.6 1.4 bitcast_convert_fusion.5
  261.6 2.6 convolution_convert_fusion
  264.3 1.4 bitcast_convert_fusion.4
  270.4 1.8 bitcast_convert_fusion.2
  272.3 1.9 constant_dynamic-update-slice_fusion.9
  274.2 3.5 reduce-scatter.9.cloned.1.call-done
  280.3 3.2 convolution_add_fusion.2
  283.5 90.4 %reduce-scatter.5.cloned.1.call-done = bf16[1,1024,768]{2,1,0:T(8,128)(2,1)} async-done(((bf16[8,1024,768]{2,1,0:T(8,128)(2,1)}), bf16[1,1024,768]{2,1,0:T(8,128)(2,1)}) %reduce-scatter.5.cloned.1.call-update) | async-done | bytes 1572880 | tf_op jit(solution)/shard_map/reduce_scatter | solution.py:128
  374.0 3.4 fusion.15
  377.7 13.4 %all-reduce.1 = bf16[8,288]{1,0:T(8,128)(2,1)S(1)} all-reduce(bf16[8,288]{1,0:T(8,128)(2,1)S(1)} %pad_maximum_fusion.4), channel_id=5, replica_groups=mesh['dp'=4,'fsdp'=8] {'fsdp'}, use_global_device_ids=true, to_apply=%region_15.16.clone | all-reduce | flops 2304 | bytes 9216
  391.8 11.7 %all-reduce.2 = bf16[288]{0:T(512)(128)(2,1)S(1)} all-reduce(bf16[288]{0:T(512)(128)(2,1)S(1)} %dynamic-slice_reduce_fusion), channel_id=6, replica_groups=mesh['dp'=4,'fsdp'=8] {'dp'}, use_global_device_ids=true, to_apply=%region_16.17.clone | all-reduce | flops 288 | bytes 1152
  403.8 3.3 fusion.49
  407.2 2.1 fusion.11
  409.3 3.1 convolution_add_fusion
  414.2 2.8 collective-permute-done.1
  417.2 1.3 collective-permute-start.4
  419.1 14.5 %collective-permute-done.4 = bf16[48,2048]{1,0:T(8,128)(2,1)S(1)} collective-permute-done((bf16[48,2048]{1,0:T(8,128)(2,1)}, bf16[48,2048]{1,0:T(8,128)(2,1)S(1)}, u32[]{:S(2)}, u32[]{:S(2)}) %collective-permute-start.4) | collective-permute-done | bytes 196640 | tf_op jit(solution)/shard_map/ppermute | solution.py:18
  434.6 1.8 collective-permute-start.5
  436.4 1.6 constant_dynamic-update-slice_fusion.29
  438.7 5.9 %reduce-scatter.7.cloned.1.call-done = bf16[256,768]{1,0:T(8,128)(2,1)} async-done(((bf16[1024,768]{1,0:T(8,128)(2,1)}), bf16[256,768]{1,0:T(8,128)(2,1)}) %reduce-scatter.7.cloned.1.call-update) | async-done | bytes 393232 | tf_op jit(solution)/shard_map/reduce_scatter | solution.py:129
  444.6 2.4 collective-permute-start.2
  447.0 9.7 %collective-permute-done.5 = bf16[96,2048]{1,0:T(8,128)(2,1)S(1)} collective-permute-done((bf16[96,2048]{1,0:T(8,128)(2,1)S(1)}, bf16[96,2048]{1,0:T(8,128)(2,1)S(1)}, u32[]{:S(2)}, u32[]{:S(2)}) %collective-permute-start.5) | collective-permute-done | bytes 393248 | tf_op jit(solution)/shard_map/ppermute | solution.py:18
  458.2 7.2 %collective-permute-done.2 = bf16[256,768]{1,0:T(8,128)(2,1)S(1)} collective-permute-done((bf16[256,768]{1,0:T(8,128)(2,1)}, bf16[256,768]{1,0:T(8,128)(2,1)S(1)}, u32[]{:S(2)}, u32[]{:S(2)}) %collective-permute-start.2) | collective-permute-done | bytes 393248 | tf_op jit(solution)/shard_map/ppermute | solution.py:18
  466.4 6.7 %collective-permute-start.3 = (bf16[512,768]{1,0:T(8,128)(2,1)S(1)}, bf16[512,768]{1,0:T(8,128)(2,1)S(1)}, u32[]{:S(2)}, u32[]{:S(2)}) collective-permute-start(bf16[512,768]{1,0:T(8,128)(2,1)S(1)} %pad_maximum_fusion.2), channel_id=1, source_target_pairs={{0,16},{8,24},{16,0},{24,8},{1,17},{9,25},{17,1},{25,9},{2,18},{10... | collective-permute-start | bytes 2359304 | tf_op jit(solution)/shard_map/ppermute | solution.py:18
  474.5 2.5 dynamic-slice_convert_fusion.1
  477.0 29.1 %collective-permute-done.3 = bf16[512,768]{1,0:T(8,128)(2,1)S(1)} collective-permute-done((bf16[512,768]{1,0:T(8,128)(2,1)S(1)}, bf16[512,768]{1,0:T(8,128)(2,1)S(1)}, u32[]{:S(2)}, u32[]{:S(2)}) %collective-permute-start.3) | collective-permute-done | bytes 786464 | tf_op jit(solution)/shard_map/ppermute | solution.py:18
  507.3 1.4 dynamic-slice_convert_fusion.3
  (298 shorter events, 60.3 us)
Async XLA Ops:
  7.2 149.8 %copy-start = (bf16[2,512,768]{2,1,0:T(8,128)(2,1)S(1)}, bf16[2,512,768]{2,1,0:T(8,128)(2,1)}, u32[]{:S(2)}) copy-start(bf16[2,512,768]{2,1,0:T(8,128)(2,1)} %param.20) | copy-start | bytes 4718596
  7.2 3.1 copy-start.65
  7.2 3.7 copy-start.66
  7.2 4.4 copy-start.67
  7.2 5.1 copy-start.68
  7.3 5.7 %copy-start.69 = (bf16[96,768]{1,0:T(8,128)(2,1)S(1)}, bf16[96,768]{1,0:T(8,128)(2,1)}, u32[]{:S(2)}) copy-start(bf16[96,768]{1,0:T(8,128)(2,1)} %param.31) | copy-start | bytes 442372
  7.3 51.8 %all-gather.8.cloned.1.call-start = ((), (), s32[]{:S(2)}) async-start(), calls=%async_computation.9 | async-start | bytes 7077888 | tf_op jit(solution)/shard_map/all_gather | solution.py:109
  9.5 4.2 copy-start.70
  9.5 4.8 copy-start.71
  9.5 5.5 %copy-start.58 = (bf16[256,768]{1,0:T(8,128)(2,1)S(1)}, bf16[256,768]{1,0:T(8,128)(2,1)}, u32[]{:S(2)}) copy-start(bf16[256,768]{1,0:T(8,128)(2,1)} %param.37) | copy-start | bytes 1179652
  9.6 123.6 %all-gather.6.cloned.1.call-start = ((), (), s32[]{:S(2)}) async-start(), calls=%async_computation.8 | async-start | bytes 14155776 | tf_op jit(solution)/shard_map/all_gather | solution.py:109
  13.0 3.0 copy-start.77
  13.0 4.2 copy-start.79
  13.0 4.2 copy-start.80
  13.0 4.2 copy-start.81
  13.7 20.2 %copy-start.21 = (bf16[2,176,768]{2,1,0:T(8,128)(2,1)S(1)}, bf16[2,176,768]{2,1,0:T(8,128)(2,1)}, u32[]{:S(2)}) copy-start(bf16[2,176,768]{2,1,0:T(8,128)(2,1)} %param.19) | copy-start | bytes 1622020
  15.1 19.0 %copy-start.72 = (s32[2,176]{1,0:T(2,128)S(1)}, s32[2,176]{1,0:T(2,128)}, u32[]{:S(2)}) copy-start(s32[2,176]{1,0:T(2,128)} %param.21) | copy-start | bytes 4228
  15.1 19.2 %copy-start.76 = (s32[2,512]{1,0:T(2,128)S(1)}, s32[2,512]{1,0:T(2,128)}, u32[]{:S(2)}) copy-start(s32[2,512]{1,0:T(2,128)} %param.22) | copy-start | bytes 12292
  15.9 261.8 %reduce-scatter.9.cloned.1.call-start = ((), (), s32[]{:S(2)}) async-start(), calls=%async_computation.6 | async-start | bytes 7077888 | tf_op jit(solution)/shard_map/reduce_scatter | solution.py:128
  147.6 16.0 %copy-start.17 = (bf16[2,176,768]{1,2,0:T(8,128)(2,1)}, bf16[2,176,768]{1,2,0:T(8,128)(2,1)S(1)}, u32[]{:S(2)}) copy-start(bf16[2,176,768]{1,2,0:T(8,128)(2,1)S(1)} %copy.106) | copy-start | bytes 1622020
  157.0 4.0 copy-start.25
  173.0 3.5 copy-start.32
  176.5 3.4 copy-start.1
  176.5 3.4 copy-start.49
  179.7 2.8 copy-start.59
  180.0 2.6 copy-start.8
  183.4 20.8 %copy-start.9 = (f32[2,176,768]{2,1,0:T(8,128)}, f32[2,176,768]{2,1,0:T(8,128)S(1)}, u32[]{:S(2)}) copy-start(f32[2,176,768]{2,1,0:T(8,128)S(1)} %get-tuple-element.61) | copy-start | bytes 3244036
  215.8 158.1 %reduce-scatter.5.cloned.1.call-start = ((), (), s32[]{:S(2)}) async-start(), calls=%async_computation.4 | async-start | bytes 14155776 | tf_op jit(solution)/shard_map/reduce_scatter | solution.py:128
  215.9 7.8 %slice-start = ((s8[8650752]{0:T(1024)(128)(4,1)}), s8[4194304]{0:T(1024)(128)(4,1)S(1)}, s32[]{:S(2)}) async-start(s8[8650752]{0:T(1024)(128)(4,1)} %bitcast.191), calls=%async_computation.10 | async-start | bytes 8388608
  215.9 7.8 %slice-start.1 = ((s8[8650752]{0:T(1024)(128)(4,1)}), s8[4194304]{0:T(1024)(128)(4,1)S(1)}, s32[]{:S(2)}) async-start(s8[8650752]{0:T(1024)(128)(4,1)} %bitcast.191), calls=%async_computation.11 | async-start | bytes 8388608
  215.9 7.8 %slice-start.2 = ((s8[8650752]{0:T(1024)(128)(4,1)}), s8[262144]{0:T(1024)(128)(4,1)S(1)}, s32[]{:S(2)}) async-start(s8[8650752]{0:T(1024)(128)(4,1)} %bitcast.191), calls=%async_computation.12 | async-start | bytes 524288
  215.9 7.8 %copy-start.33 = (pred[2,176,512]{2,1,0:T(8,128)(4,1)S(1)}, pred[2,176,512]{2,1,0:T(8,128)(4,1)}, u32[]{:S(2)}) copy-start(pred[2,176,512]{2,1,0:T(8,128)(4,1)} %broadcast_compare_fusion) | copy-start | bytes 540676
  215.9 7.8 %copy-start.60 = (f32[2,12,176]{2,1,0:T(8,128)S(1)}, f32[2,12,176]{2,1,0:T(8,128)}, u32[]{:S(2)}) copy-start(f32[2,12,176]{2,1,0:T(8,128)} %copy-done.59) | copy-start | bytes 50692
  223.7 2.7 copy-start.20
  235.5 4.4 slice-start.6
  235.5 4.4 slice-start.7
  235.5 4.4 copy-start.63
  249.9 6.4 %slice-start.8 = ((s8[4325376]{0:T(1024)(128)(4,1)}), s8[4194304]{0:T(1024)(128)(4,1)S(1)}, s32[]{:S(2)}) async-start(s8[4325376]{0:T(1024)(128)(4,1)} %bitcast.197), calls=%async_computation.18 | async-start | bytes 8388608
  252.6 3.7 slice-start.9
  256.6 3.5 slice-start.3
  256.6 4.5 slice-start.4
  257.6 3.6 slice-start.5
  274.2 3.7 copy-start.84
  274.2 5.0 copy-start.29
  274.2 5.0 copy-start.43
  274.2 143.0 %reduce-scatter.11.cloned.1.call-start = ((), (), s32[]{:S(2)}) async-start(), calls=%async_computation.7 | async-start | bytes 983040 | tf_op jit(solution)/shard_map/reduce_scatter | solution.py:129
  277.8 166.8 %reduce-scatter.7.cloned.1.call-start = ((), (), s32[]{:S(2)}) async-start(), calls=%async_computation.5 | async-start | bytes 1966080 | tf_op jit(solution)/shard_map/reduce_scatter | solution.py:129
  280.3 93.7 %copy-start.27 = (bf16[8,96,768]{2,1,0:T(8,128)(2,1)S(1)}, bf16[8,96,768]{2,1,0:T(8,128)(2,1)}, u32[]{:S(2)}) copy-start(bf16[8,96,768]{2,1,0:T(8,128)(2,1)} %get-tuple-element.30) | copy-start | bytes 3538948
  283.5 90.5 %copy-start.24 = (bf16[2,176,768]{2,1,0:T(8,128)(2,1)S(1)}, bf16[2,176,768]{2,1,0:T(8,128)(2,1)}, u32[]{:S(2)}) copy-start(bf16[2,176,768]{2,1,0:T(8,128)(2,1)} %param.19) | copy-start | bytes 1622020
  374.0 3.4 copy-start.78
  374.0 3.5 copy-start.73
  403.5 3.6 copy-start.10
  403.5 3.6 copy-start.41
  403.6 3.6 copy-start.86
  403.6 8.9 %collective-permute-start = (bf16[72]{0:T(256)(128)(2,1)S(1)}, bf16[72]{0:T(256)(128)(2,1)S(1)}, u32[]{:S(2)}, u32[]{:S(2)}) collective-permute-start(bf16[72]{0:T(256)(128)(2,1)S(1)} %dynamic-slice.4), channel_id=1, source_target_pairs={{0,24},{8,0},{16,8},{24,16},{1,25},{9,1},{17,9},{25,17},{2,26},{10... | collective-permute-start | bytes 440 | tf_op jit(solution)/shard_map/ppermute | solution.py:18
  409.3 3.6 copy-start.13
  409.3 3.6 copy-start.35
  412.6 4.5 collective-permute-start.1
  417.2 40.3 %copy-start.48 = (bf16[48,2048]{1,0:T(8,128)(2,1)S(1)}, bf16[48,2048]{1,0:T(8,128)(2,1)}, u32[]{:S(2)}) copy-start(bf16[48,2048]{1,0:T(8,128)(2,1)} %reduce-scatter.11.cloned.1.call-done) | copy-start | bytes 589828
  417.2 16.4 %collective-permute-start.4 = (bf16[48,2048]{1,0:T(8,128)(2,1)}, bf16[48,2048]{1,0:T(8,128)(2,1)S(1)}, u32[]{:S(2)}, u32[]{:S(2)}) collective-permute-start(bf16[48,2048]{1,0:T(8,128)(2,1)} %reduce-scatter.11.cloned.1.call-done), channel_id=1, source_target_pairs={{0,24},{8,0},{16,8},{24,16},{1,25},{9,1},{17,9},{25,17},{2,26},{10... | collective-permute-start | bytes 589832 | tf_op jit(solution)/shard_map/ppermute | solution.py:18
  434.6 22.1 %collective-permute-start.5 = (bf16[96,2048]{1,0:T(8,128)(2,1)S(1)}, bf16[96,2048]{1,0:T(8,128)(2,1)S(1)}, u32[]{:S(2)}, u32[]{:S(2)}) collective-permute-start(bf16[96,2048]{1,0:T(8,128)(2,1)S(1)} %pad_maximum_fusion.3), channel_id=1, source_target_pairs={{0,16},{8,24},{16,0},{24,8},{1,17},{9,25},{17,1},{25,9},{2,18},{10... | collective-permute-start | bytes 1179656 | tf_op jit(solution)/shard_map/ppermute | solution.py:18
  444.6 20.7 %collective-permute-start.2 = (bf16[256,768]{1,0:T(8,128)(2,1)}, bf16[256,768]{1,0:T(8,128)(2,1)S(1)}, u32[]{:S(2)}, u32[]{:S(2)}) collective-permute-start(bf16[256,768]{1,0:T(8,128)(2,1)} %reduce-scatter.7.cloned.1.call-done), channel_id=1, source_target_pairs={{0,24},{8,0},{16,8},{24,16},{1,25},{9,1},{17,9},{25,17},{2,26},{10... | collective-permute-start | bytes 1179656 | tf_op jit(solution)/shard_map/ppermute | solution.py:18
  466.4 39.7 %collective-permute-start.3 = (bf16[512,768]{1,0:T(8,128)(2,1)S(1)}, bf16[512,768]{1,0:T(8,128)(2,1)S(1)}, u32[]{:S(2)}, u32[]{:S(2)}) collective-permute-start(bf16[512,768]{1,0:T(8,128)(2,1)S(1)} %pad_maximum_fusion.2), channel_id=1, source_target_pairs={{0,16},{8,24},{16,0},{24,8},{1,17},{9,25},{17,1},{25,9},{2,18},{10... | collective-permute-start | bytes 2359304 | tf_op jit(solution)/shard_map/ppermute | solution.py:18
  473.7 3.3 copy-start.36
  (45 other events, 73.4 us)
Sparse Core Ops, SparseCore 0:
  10.6 48.4 all-gather.7
  61.0 72.1 all-gather.5
  216.0 61.7 reduce-scatter.8
  281.5 92.3 reduce-scatter.4
  376.2 23.3 reduce-scatter.10
  401.9 42.6 reduce-scatter.6
